TPU v7x, 32 devices: a whole 2x2x4 slice. The times are simulated.
32 devices in a mesh: dp: 8 (over z, y), tensor: 4 (over x, core).
Axes of the slice: x: 2, y: 2, z: 4, core: 2. Of those that a mesh axis runs over, the one named last changes fastest.
Arguments:
- query: bfloat16 [64, 64, 128], P('dp', 'tensor'), may hold values from -8 to 8
- kv_pages: bfloat16 [560, 8, 2, 128, 128], P('dp', 'tensor'), may hold values from -8 to 8
- move_plan: int32 [8, 3, 12], P('dp'), may hold values from 0 to 69, as said below
- move_count: int32 [8], P('dp'), may hold values from 9 to 12
- block_table: int32 [64, 8], P('dp'), may hold values from 0 to 69, as said below
- seq_lens: int32 [64], P('dp'), may hold values from 1 to 1024
- out_weight: bfloat16 [8192, 8192], P('tensor', 'dp'), may hold values from -0.0625 to 0.0625
Outputs:
- new_pages: bfloat16 [560, 8, 2, 128, 128], P('dp', 'tensor')
- projected: bfloat16 [64, 8192], P(None, 'dp')
Inputs may be any that keep to these rules, and one draw needn't show every extreme that they name: `move_plan`: row 0 holds the device's own source slots, distinct within a device; row 1 target devices; row 2 target slots. Entries at or past the device's move_count are padding to be ignored. At most 2 valid moves go from one device to one device, and some pair has exactly 2. The (target device, target slot) pairs of all valid moves are distinct. `block_table`: all entries of the sequences of one device are distinct slots of that device; sequence s belongs to device s // 8.
All inputs are finite; a program needn't handle non-finite values.
Results may differ from a plain program's by a relative error of at most 0.0055.
Values may be sent and summed in bfloat16 or wider, within the bound.
No kernel may reach another device: no remote copies, remote signals or barrier semaphores. Data moves between devices by JAX's collectives and lax.ppermute only.
A program may use at most 128 MiB of HBM per device.

v0:
```python
import math
import jax
import jax.numpy as jnp
from jax import lax
from jax.sharding import PartitionSpec as P

HD = 128
BLOCK = 128
BLOCKS = 8
CAP = 2


def body(query, kv_pages, move_plan, move_count, block_table, seq_lens, out_weight):
    slots_here = kv_pages.shape[0]
    move_total = move_plan.shape[2]
    devices = lax.axis_size("dp")
    capacity = CAP
    holding_rows = devices * capacity
    move_list = move_plan[0]
    move_index = jnp.arange(move_total, dtype=jnp.int32)
    is_valid = move_index < move_count[0]
    target_dev = move_list[1]
    earlier = (
        (target_dev[:, None] == target_dev[None, :])
        & is_valid[None, :]
        & (move_index[None, :] < move_index[:, None])
    )
    dest_rank = jnp.sum(earlier.astype(jnp.int32), axis=1)
    send_row = jnp.where(is_valid, target_dev * capacity + dest_rank, -1)
    flat_pages = kv_pages.reshape(slots_here, -1)
    picked = flat_pages[move_list[0]]
    select = jnp.arange(holding_rows, dtype=jnp.int32)[:, None] == send_row[None, :]
    outgoing = jnp.dot(
        select.astype(jnp.bfloat16), picked, preferred_element_type=jnp.float32
    ).astype(jnp.bfloat16)
    outgoing = outgoing.reshape((holding_rows,) + kv_pages.shape[1:])
    out_slots = jnp.sum(select.astype(jnp.int32) * (move_list[2][None, :] + 1), axis=1) - 1
    slot_tags = out_slots.astype(jnp.float32).astype(jnp.bfloat16)
    arrived, arrived_tags = (
        lax.all_to_all(outgoing, "dp", split_axis=0, concat_axis=0, tiled=True),
        lax.all_to_all(slot_tags, "dp", split_axis=0, concat_axis=0, tiled=True),
    )
    incoming = arrived_tags.astype(jnp.float32).astype(jnp.int32)
    hit_table = jnp.arange(slots_here, dtype=jnp.int32)[:, None] == incoming[None, :]
    placed = jnp.dot(
        hit_table.astype(jnp.bfloat16),
        arrived.reshape(holding_rows, -1),
        preferred_element_type=jnp.float32,
    ).astype(jnp.bfloat16)
    written = jnp.any(hit_table, axis=1)
    new_pages = jnp.where(written[:, None], placed, flat_pages).reshape(kv_pages.shape)
    seq_here = query.shape[0]
    local_heads = new_pages.shape[1]
    head_dim = query.shape[2]
    group_size = query.shape[1] // local_heads
    context = BLOCKS * BLOCK
    gathered = new_pages[block_table]
    key_rows = jnp.transpose(gathered[:, :, :, 0], (0, 2, 1, 3, 4)).reshape(
        seq_here, local_heads, context, head_dim
    )
    value_rows = jnp.transpose(gathered[:, :, :, 1], (0, 2, 1, 3, 4)).reshape(
        seq_here, local_heads, context, head_dim
    )
    grouped = query.reshape(seq_here, local_heads, group_size, head_dim)
    score_scale = 1.0 / math.sqrt(HD)
    scores = (
        jnp.einsum("skgd,sktd->skgt", grouped, key_rows, preferred_element_type=jnp.float32)
        * score_scale
    )
    position = jnp.arange(context, dtype=jnp.int32)
    scores = jnp.where(position[None, None, None, :] < seq_lens[:, None, None, None], scores, -1e30)
    largest = jnp.max(scores, axis=-1, keepdims=True)
    expo = jnp.exp(scores - largest)
    weights = (expo / jnp.sum(expo, axis=-1, keepdims=True)).astype(jnp.bfloat16)
    mixed_heads = jnp.einsum(
        "skgt,sktd->skgd", weights, value_rows, preferred_element_type=jnp.float32
    )
    attention = mixed_heads.reshape(seq_here, local_heads * group_size * head_dim).astype(
        jnp.bfloat16
    )
    partial_sums = jnp.dot(
        lax.all_gather(attention, "dp", axis=0, tiled=True),
        out_weight,
        preferred_element_type=jnp.float32,
    )
    summed = lax.psum(partial_sums, "tensor")
    return (new_pages, summed.astype(jnp.bfloat16))


def solution(mesh):
    placed = (
        P("dp", "tensor", None),
        P("dp", "tensor", None, None, None),
        P("dp", None, None),
        P("dp"),
        P("dp", None),
        P("dp"),
        P("tensor", "dp"),
    )
    return jax.shard_map(
        body,
        mesh=mesh,
        in_specs=placed,
        out_specs=(P("dp", "tensor", None, None, None), P(None, "dp")),
        check_vma=False,
    )
```

profile of v0, /device:TPU:1, one launch (start us, length us, event | category | flops | bytes accessed | tf_op | source)
XLA Modules:
  0.0 194.9 jit_solution(8297206147046076033)
XLA Ops:
  0.6 0.0 copy-start
  0.6 0.7 slice_bitcast_fusion
  2.0 0.2 convert_reduce_fusion
  2.2 0.7 add_select_fusion
  2.8 0.1 select_reduce_fusion
  3.0 0.7 convert_element_type.79
  3.7 6.4 %all-to-all-start = ((bf16[8,2,1]{1,2,0:T(2,128)(2,1)}), bf16[8,2,1]{1,2,0:T(2,128)(2,1)S(1)}, u32[]{:S(2)}, u32[]{:S(2)}) async-start(bf16[8,2,1]{1,2,0:T(2,128)(2,1)} %convert_element_type.79), calls=%async_computation | async-start | bytes 8192 | tf_op jit(solution)/shard_map/all_to_all | solution.py:41
  10.0 0.7 fusion.16
  10.7 8.8 %pad.2 = bf16[72,512,128]{2,1,0:T(8,128)(2,1)} pad(bf16[70,512,128]{2,1,0:T(8,128)(2,1)} %bitcast.69, bf16[]{:T(256)} %constant.38), padding=0_2x0_0x0_0 | pad | bytes 18612226
  19.5 13.8 %copy.21 = bf16[9,8,512,128]{3,1,2,0:T(8,128)(2,1)} copy(bf16[9,8,512,128]{3,2,1,0:T(8,128)(2,1)} %bitcast.62) | data formatting | bytes 18874368
  33.3 7.8 %gather_fusion = bf16[12,65536]{1,0:T(8,128)(2,1)S(1)} fusion(bf16[70,65536]{1,0:T(8,128)(2,1)} %bitcast.59, s32[1024]{0:T(1024)S(1)} %pad_clamp_fusion.1), kind=kCustom, calls=%fused_computation | custom fusion | bytes 3145776 | tf_op jit(solution)/shard_map/gather | solution.py:31
  41.1 0.7 fusion.4
  41.8 0.0 copy-start.1
  41.8 0.0 copy-start.2
  41.8 1.9 copy.22
  43.7 0.0 all-to-all-done
  43.7 5.4 %all-to-all-start.1 = ((bf16[16,2,2,128,128]{4,3,2,1,0:T(8,128)(2,1)}), bf16[16,2,2,128,128]{4,3,2,1,0:T(8,128)(2,1)S(1)}, u32[]{:S(2)}, u32[]{:S(2)}) async-start(bf16[16,2,2,128,128]{4,3,2,1,0:T(8,128)(2,1)} %bitcast.24), calls=%async_computation.1 | async-start | bytes 4194304 | tf_op jit(solution)/shard_map/all_to_all | solution.py:40
  49.2 0.0 copy-done.1
  49.2 0.1 reshape.158
  49.3 0.0 copy-done.2
  49.3 0.1 iota_compare_fusion
  49.4 0.1 convert_element_type.72
  49.4 0.1 fusion.12
  49.5 46.5 %all-to-all-done.1 = bf16[16,2,2,128,128]{4,3,2,1,0:T(8,128)(2,1)S(1)} async-done(((bf16[16,2,2,128,128]{4,3,2,1,0:T(8,128)(2,1)}), bf16[16,2,2,128,128]{4,3,2,1,0:T(8,128)(2,1)S(1)}, u32[]{:S(2)}, u32[]{:S(2)}) %all-to-all-start.1) | async-done | bytes 2097184 | tf_op jit(solution)/shard_map/all_to_all | solution.py:40
  96.0 10.8 %fusion.1 = bf16[70,65536]{1,0:T(8,128)(2,1)} fusion(bf16[70,65536]{1,0:T(8,128)(2,1)} %bitcast.60, pred[70]{0:T(512)(128)(4,1)S(1)} %fusion.12, bf16[2,8,512,128]{3,2,1,0:T(8,128)(2,1)S(1)} %bitcast.70, s32[16]{0:T(128)S(1)} %convert_element_type.72), kind=kOutput, calls=%fused_computation.4 | convolution fusion | flops 155976800 | bytes 20447366 | tf_op jit(solution)/shard_map/dot_general | solution.py:45
  106.8 9.9 %copy.24 = bf16[9,8,512,128]{3,2,1,0:T(8,128)(2,1)} copy(bf16[9,8,512,128]{3,1,2,0:T(8,128)(2,1)} %bitcast.61) | data formatting | bytes 18874368
  116.7 8.4 %slice.29 = bf16[70,512,128]{2,1,0:T(8,128)(2,1)} slice(bf16[72,512,128]{2,1,0:T(8,128)(2,1)} %bitcast.63), slice={[0:70], [0:512], [0:128]} | slice | bytes 18350080
  125.1 9.1 %gather_fusion.1 = bf16[64,2,2,128,128]{4,3,2,1,0:T(8,128)(2,1)} fusion(bf16[70,2,2,128,128]{4,3,2,1,0:T(8,128)(2,1)} %bitcast.64, s32[1024]{0:T(1024)S(1)} %pad_clamp_fusion), kind=kCustom, calls=%fused_computation.1 | custom fusion | bytes 16777472 | tf_op jit(solution)/shard_map/gather | solution.py:57
  134.2 3.8 %fusion.17 = (bf16[8,8,2,1,128,128]{5,4,3,2,1,0:T(8,128)(2,1)S(1)}, bf16[8,8,2,1,128,128]{5,4,3,2,1,0:T(8,128)(2,1)S(1)}) fusion(bf16[8,8,2,2,128,128]{5,4,3,2,1,0:T(8,128)(2,1)} %bitcast.66), kind=kLoop, calls=%fused_computation.41 | loop fusion | bytes 16777216 | tf_op jit(solution)/shard_map/slice | solution.py:58
  138.1 0.6 copy.19
  138.6 0.0 copy-done
  138.7 1.2 fusion.8
  139.8 0.3 fusion.18
  140.1 2.2 %copy.20 = bf16[8,8,2,1,128,128]{5,4,1,2,0,3:T(8,128)(2,1)} copy(bf16[8,8,2,1,128,128]{5,4,3,2,1,0:T(8,128)(2,1)S(1)} %get-tuple-element.3) | data formatting | bytes 8388608
  142.3 2.9 %fusion.9 = bf16[1,8,16,128]{3,2,1,0:T(8,128)(2,1)S(1)} fusion(bf16[8,2,1024,128]{3,2,1,0:T(8,128)(2,1)} %bitcast.67, f32[8,2,8]{2,1,0:T(2,128)S(1)} %fusion.18, f32[8,2,8,1024]{3,2,1,0:T(8,128)S(1)} %fusion.8), kind=kOutput, calls=%fused_computation.15 | convolution fusion | flops 33965184 | bytes 4751872 | tf_op jit(solution)/shard_map/skgt,sktd->skgd/dot_general | solution.py:75
  145.3 25.4 %all_gather.3 = bf16[64,2048]{1,0:T(8,128)(2,1)S(1)} all-gather(bf16[8,2048]{1,0:T(8,128)(2,1)S(1)} %bitcast.71), channel_id=1, replica_groups=mesh['dp'=8,'tensor'=4] {'dp'}, dimensions={0}, use_global_device_ids=true | all-gather | bytes 294912 | tf_op jit(solution)/shard_map/all_gather | solution.py:82
  170.7 3.0 %fusion.19 = f32[64,1024]{1,0:T(8,128)S(1)} fusion(bf16[64,2048]{1,0:T(8,128)(2,1)S(1)} %all_gather.3, bf16[2048,1024]{1,0:T(8,128)(2,1)} %param.13), kind=kOutput, calls=%fused_computation.43 | convolution fusion | flops 268435456 | bytes 4718592 | tf_op jit(solution)/shard_map/dot_general | solution.py:81
  173.7 21.2 %all-reduce.1 = bf16[64,1024]{1,0:T(8,128)(2,1)} all-reduce(f32[64,1024]{1,0:T(8,128)S(1)} %fusion.19), channel_id=1, replica_groups=mesh['dp'=8,'tensor'=4] {'tensor'}, use_global_device_ids=true, to_apply=%region_5.6 | all-reduce | flops 65536 | bytes 393216 | tf_op jit(solution)/shard_map/psum | solution.py:86
  (7 shorter events, 0.1 us)
Async XLA Ops:
  0.6 138.0 %copy-start = (bf16[8,16,128]{2,1,0:T(8,128)(2,1)S(1)}, bf16[8,16,128]{2,1,0:T(8,128)(2,1)}, u32[]{:S(2)}) copy-start(bf16[8,16,128]{2,1,0:T(8,128)(2,1)} %param.7) | copy-start | bytes 98308
  3.7 40.1 %all-to-all-start = ((bf16[8,2,1]{1,2,0:T(2,128)(2,1)}), bf16[8,2,1]{1,2,0:T(2,128)(2,1)S(1)}, u32[]{:S(2)}, u32[]{:S(2)}) async-start(bf16[8,2,1]{1,2,0:T(2,128)(2,1)} %convert_element_type.79), calls=%async_computation | async-start | bytes 8192 | tf_op jit(solution)/shard_map/all_to_all | solution.py:41
  41.8 7.3 %copy-start.1 = (s32[8,8]{1,0:T(8,128)S(1)}, s32[8,8]{1,0:T(8,128)}, u32[]{:S(2)}) copy-start(s32[8,8]{1,0:T(8,128)} %param.11) | copy-start | bytes 772
  41.8 7.4 %copy-start.2 = (s32[8]{0:T(128)S(1)}, s32[8]{0:T(128)}, u32[]{:S(2)}) copy-start(s32[8]{0:T(128)} %param.12) | copy-start | bytes 100
  43.7 52.3 %all-to-all-start.1 = ((bf16[16,2,2,128,128]{4,3,2,1,0:T(8,128)(2,1)}), bf16[16,2,2,128,128]{4,3,2,1,0:T(8,128)(2,1)S(1)}, u32[]{:S(2)}, u32[]{:S(2)}) async-start(bf16[16,2,2,128,128]{4,3,2,1,0:T(8,128)(2,1)} %bitcast.24), calls=%async_computation.1 | async-start | bytes 4194304 | tf_op jit(solution)/shard_map/all_to_all | solution.py:40
where the time goes:
time: 196 us; the launch traced here: 195 us
  local copies, waits for them, and re-layouts  67.2 us (34%)
  blocking collectives  46.6 us (24%)
  waiting for transfers between devices  46.5 us (24%)
  matrix products  18.6 us (9%)
  starting transfers between devices  11.8 us (6%)
  other arithmetic  2.78 us (1%)
    all_to_all x1, waiting for transfers between devices, body(): lax.all_to_all(outgoing, 'dp', split_axis=0, concat_axis=0, tiled=True)  46.5 us
    unnamed x14, local copies, waits for them, and re-layouts  45.6 us
    all_gather x1, blocking collectives, body(): lax.all_gather(attention, 'dp', axis=0, tiled=True)  25.4 us
    psum x1, blocking collectives, body(): summed = lax.psum(partial_sums, 'tensor')  21.2 us
    dot_general x1, matrix products, body(): jnp.dot(hit_table.astype(jnp.bfloat16), arrived.reshape(holding_rows, -1)...  10.8 us
    gather x1, local copies, waits for them, and re-layouts, body(): gathered = new_pages[block_table]  9.14 us
    gather x1, local copies, waits for them, and re-layouts, body(): picked = flat_pages[move_list[0]]  7.81 us
    all_to_all x1, starting transfers between devices, body(): lax.all_to_all(slot_tags, 'dp', split_axis=0, concat_axis=0, tiled=True)  6.37 us
  transfers between devices with their start and end apart: 2, of which 1 were waited for; matrix products, arithmetic and copies ran while one was open for 17% of the time, Pallas kernels for 0%

commit v1 on v0

--- a/solution.py
+++ b/solution.py
@@ -83,7 +83,9 @@
         out_weight,
         preferred_element_type=jnp.float32,
     )
-    summed = lax.psum(partial_sums, "tensor")
+    summed = partial_sums
+    for hop in (1, 2):
+        summed = summed + lax.ppermute(summed, "tensor", [(dev, dev ^ hop) for dev in range(4)])
     return (new_pages, summed.astype(jnp.bfloat16))
 
 

time: 196 us -> 193 us (0.985)
  blocking collectives: 46.6 us -> 25.4 us
  starting transfers between devices: 11.8 us -> 20.8 us
  waiting for transfers between devices: 46.5 us -> 53.9 us
    psum x1 -> x0, blocking collectives: 21.2 us -> none  [body(): summed = lax.psum(partial_sums, 'tensor')]
    ppermute x0 -> x2, starting transfers between devices: none -> 9.01 us  [body(): lax.ppermute(summed, 'tensor', [(dev, dev ^ hop) for dev in range(4)])]
    ppermute x0 -> x2, waiting for transfers between devices: none -> 7.44 us  [body(): lax.ppermute(summed, 'tensor', [(dev, dev ^ hop) for dev in range(4)])]
  transfers between devices with their start and end apart: 2 -> 4, of which waited for: 1 -> 3; matrix products, arithmetic and copies ran while one was open for 17% -> 18% of each run, Pallas kernels for 0% -> 0%
where the time goes in v1:
time: 193 us; the launch traced here: 191 us
  local copies, waits for them, and re-layouts  67.2 us (35%)
  waiting for transfers between devices  53.9 us (28%)
  blocking collectives  25.4 us (13%)
  starting transfers between devices  20.8 us (11%)
  matrix products  18.6 us (10%)
  other arithmetic  3.51 us (2%)
    all_to_all x1, waiting for transfers between devices, body(): lax.all_to_all(outgoing, 'dp', split_axis=0, concat_axis=0, tiled=True)  46.5 us
    unnamed x14, local copies, waits for them, and re-layouts  45.6 us
    all_gather x1, blocking collectives, body(): lax.all_gather(attention, 'dp', axis=0, tiled=True)  25.4 us
    dot_general x1, matrix products, body(): jnp.dot(hit_table.astype(jnp.bfloat16), arrived.reshape(holding_rows, -1)...  10.8 us
    gather x1, local copies, waits for them, and re-layouts, body(): gathered = new_pages[block_table]  9.14 us
    ppermute x2, starting transfers between devices, body(): lax.ppermute(summed, 'tensor', [(dev, dev ^ hop) for dev in range(4)])  9.01 us
    gather x1, local copies, waits for them, and re-layouts, body(): picked = flat_pages[move_list[0]]  7.81 us
    ppermute x2, waiting for transfers between devices, body(): lax.ppermute(summed, 'tensor', [(dev, dev ^ hop) for dev in range(4)])  7.44 us
  transfers between devices with their start and end apart: 4, of which 3 were waited for; matrix products, arithmetic and copies ran while one was open for 18% of the time, Pallas kernels for 0%

profile of v1, /device:TPU:1, one launch (start us, length us, event | category | flops | bytes accessed | tf_op | source)
XLA Modules:
  0.0 190.9 jit_solution(7469304974899114664)
XLA Ops:
  0.6 0.0 copy-start
  0.6 0.7 slice_bitcast_fusion
  2.0 0.2 convert_reduce_fusion
  2.2 0.7 add_select_fusion
  2.8 0.1 select_reduce_fusion
  3.0 0.7 convert_element_type.79
  3.7 6.4 %all-to-all-start = ((bf16[8,2,1]{1,2,0:T(2,128)(2,1)}), bf16[8,2,1]{1,2,0:T(2,128)(2,1)S(1)}, u32[]{:S(2)}, u32[]{:S(2)}) async-start(bf16[8,2,1]{1,2,0:T(2,128)(2,1)} %convert_element_type.79), calls=%async_computation | async-start | bytes 8192 | tf_op jit(solution)/shard_map/all_to_all | solution.py:41
  10.0 0.7 fusion.16
  10.7 8.8 %pad.2 = bf16[72,512,128]{2,1,0:T(8,128)(2,1)} pad(bf16[70,512,128]{2,1,0:T(8,128)(2,1)} %bitcast.69, bf16[]{:T(256)} %constant.38), padding=0_2x0_0x0_0 | pad | bytes 18612226
  19.5 13.8 %copy.21 = bf16[9,8,512,128]{3,1,2,0:T(8,128)(2,1)} copy(bf16[9,8,512,128]{3,2,1,0:T(8,128)(2,1)} %bitcast.62) | data formatting | bytes 18874368
  33.3 7.8 %gather_fusion = bf16[12,65536]{1,0:T(8,128)(2,1)S(1)} fusion(bf16[70,65536]{1,0:T(8,128)(2,1)} %bitcast.59, s32[1024]{0:T(1024)S(1)} %pad_clamp_fusion.1), kind=kCustom, calls=%fused_computation | custom fusion | bytes 3145776 | tf_op jit(solution)/shard_map/gather | solution.py:31
  41.1 0.7 fusion.4
  41.8 0.0 copy-start.1
  41.8 0.0 copy-start.2
  41.8 1.9 copy.22
  43.7 0.0 all-to-all-done
  43.7 5.4 %all-to-all-start.1 = ((bf16[16,2,2,128,128]{4,3,2,1,0:T(8,128)(2,1)}), bf16[16,2,2,128,128]{4,3,2,1,0:T(8,128)(2,1)S(1)}, u32[]{:S(2)}, u32[]{:S(2)}) async-start(bf16[16,2,2,128,128]{4,3,2,1,0:T(8,128)(2,1)} %bitcast.24), calls=%async_computation.1 | async-start | bytes 4194304 | tf_op jit(solution)/shard_map/all_to_all | solution.py:40
  49.2 0.0 copy-done.1
  49.2 0.1 reshape.158
  49.3 0.0 copy-done.2
  49.3 0.1 iota_compare_fusion
  49.4 0.1 convert_element_type.72
  49.4 0.1 fusion.12
  49.5 46.5 %all-to-all-done.1 = bf16[16,2,2,128,128]{4,3,2,1,0:T(8,128)(2,1)S(1)} async-done(((bf16[16,2,2,128,128]{4,3,2,1,0:T(8,128)(2,1)}), bf16[16,2,2,128,128]{4,3,2,1,0:T(8,128)(2,1)S(1)}, u32[]{:S(2)}, u32[]{:S(2)}) %all-to-all-start.1) | async-done | bytes 2097184 | tf_op jit(solution)/shard_map/all_to_all | solution.py:40
  96.0 10.8 %fusion.1 = bf16[70,65536]{1,0:T(8,128)(2,1)} fusion(bf16[70,65536]{1,0:T(8,128)(2,1)} %bitcast.60, pred[70]{0:T(512)(128)(4,1)S(1)} %fusion.12, bf16[2,8,512,128]{3,2,1,0:T(8,128)(2,1)S(1)} %bitcast.70, s32[16]{0:T(128)S(1)} %convert_element_type.72), kind=kOutput, calls=%fused_computation.4 | convolution fusion | flops 155976800 | bytes 20447366 | tf_op jit(solution)/shard_map/dot_general | solution.py:45
  106.8 9.9 %copy.24 = bf16[9,8,512,128]{3,2,1,0:T(8,128)(2,1)} copy(bf16[9,8,512,128]{3,1,2,0:T(8,128)(2,1)} %bitcast.61) | data formatting | bytes 18874368
  116.7 8.4 %slice.29 = bf16[70,512,128]{2,1,0:T(8,128)(2,1)} slice(bf16[72,512,128]{2,1,0:T(8,128)(2,1)} %bitcast.63), slice={[0:70], [0:512], [0:128]} | slice | bytes 18350080
  125.1 9.1 %gather_fusion.1 = bf16[64,2,2,128,128]{4,3,2,1,0:T(8,128)(2,1)} fusion(bf16[70,2,2,128,128]{4,3,2,1,0:T(8,128)(2,1)} %bitcast.64, s32[1024]{0:T(1024)S(1)} %pad_clamp_fusion), kind=kCustom, calls=%fused_computation.1 | custom fusion | bytes 16777472 | tf_op jit(solution)/shard_map/gather | solution.py:57
  134.2 3.8 %fusion.17 = (bf16[8,8,2,1,128,128]{5,4,3,2,1,0:T(8,128)(2,1)S(1)}, bf16[8,8,2,1,128,128]{5,4,3,2,1,0:T(8,128)(2,1)S(1)}) fusion(bf16[8,8,2,2,128,128]{5,4,3,2,1,0:T(8,128)(2,1)} %bitcast.66), kind=kLoop, calls=%fused_computation.42 | loop fusion | bytes 16777216 | tf_op jit(solution)/shard_map/slice | solution.py:58
  138.1 0.6 copy.19
  138.6 0.0 copy-done
  138.7 1.2 fusion.8
  139.8 0.3 fusion.18
  140.1 2.2 %copy.20 = bf16[8,8,2,1,128,128]{5,4,1,2,0,3:T(8,128)(2,1)} copy(bf16[8,8,2,1,128,128]{5,4,3,2,1,0:T(8,128)(2,1)S(1)} %get-tuple-element.3) | data formatting | bytes 8388608
  142.3 2.9 %fusion.9 = bf16[1,8,16,128]{3,2,1,0:T(8,128)(2,1)S(1)} fusion(bf16[8,2,1024,128]{3,2,1,0:T(8,128)(2,1)} %bitcast.67, f32[8,2,8]{2,1,0:T(2,128)S(1)} %fusion.18, f32[8,2,8,1024]{3,2,1,0:T(8,128)S(1)} %fusion.8), kind=kOutput, calls=%fused_computation.15 | convolution fusion | flops 33965184 | bytes 4751872 | tf_op jit(solution)/shard_map/skgt,sktd->skgd/dot_general | solution.py:75
  145.3 25.4 %all_gather.3 = bf16[64,2048]{1,0:T(8,128)(2,1)S(1)} all-gather(bf16[8,2048]{1,0:T(8,128)(2,1)S(1)} %bitcast.71), channel_id=1, replica_groups=mesh['dp'=8,'tensor'=4] {'dp'}, dimensions={0}, use_global_device_ids=true | all-gather | bytes 294912 | tf_op jit(solution)/shard_map/all_gather | solution.py:82
  170.7 3.0 %fusion.19 = f32[64,1024]{1,0:T(8,128)S(1)} fusion(bf16[64,2048]{1,0:T(8,128)(2,1)S(1)} %all_gather.3, bf16[2048,1024]{1,0:T(8,128)(2,1)} %param.13), kind=kOutput, calls=%fused_computation.44 | convolution fusion | flops 268435456 | bytes 4718592 | tf_op jit(solution)/shard_map/dot_general | solution.py:81
  173.7 7.7 %collective-permute-start = (f32[64,1024]{1,0:T(8,128)S(1)}, f32[64,1024]{1,0:T(8,128)S(1)}, u32[]{:S(2)}, u32[]{:S(2)}) collective-permute-start(f32[64,1024]{1,0:T(8,128)S(1)} %fusion.19), channel_id=1, source_target_pairs={{0,1},{1,0},{2,3},{3,2},{4,5},{5,4},{6,7},{7,6},{8,9},{9,8},{10,11... | collective-permute-start | bytes 786440 | tf_op jit(solution)/shard_map/ppermute | solution.py:88
  181.4 1.2 collective-permute-done
  182.7 1.3 collective-permute-start.1
  183.9 6.3 %collective-permute-done.1 = f32[64,1024]{1,0:T(8,128)S(1)} collective-permute-done((f32[64,1024]{1,0:T(8,128)S(1)}, f32[64,1024]{1,0:T(8,128)S(1)}, u32[]{:S(2)}, u32[]{:S(2)}) %collective-permute-start.1) | collective-permute-done | bytes 262176 | tf_op jit(solution)/shard_map/ppermute | solution.py:88
  190.2 0.7 add_convert_fusion
  (8 shorter events, 0.1 us)
Async XLA Ops:
  0.6 138.0 %copy-start = (bf16[8,16,128]{2,1,0:T(8,128)(2,1)S(1)}, bf16[8,16,128]{2,1,0:T(8,128)(2,1)}, u32[]{:S(2)}) copy-start(bf16[8,16,128]{2,1,0:T(8,128)(2,1)} %param.7) | copy-start | bytes 98308
  3.7 40.1 %all-to-all-start = ((bf16[8,2,1]{1,2,0:T(2,128)(2,1)}), bf16[8,2,1]{1,2,0:T(2,128)(2,1)S(1)}, u32[]{:S(2)}, u32[]{:S(2)}) async-start(bf16[8,2,1]{1,2,0:T(2,128)(2,1)} %convert_element_type.79), calls=%async_computation | async-start | bytes 8192 | tf_op jit(solution)/shard_map/all_to_all | solution.py:41
  41.8 7.3 %copy-start.1 = (s32[8,8]{1,0:T(8,128)S(1)}, s32[8,8]{1,0:T(8,128)}, u32[]{:S(2)}) copy-start(s32[8,8]{1,0:T(8,128)} %param.11) | copy-start | bytes 772
  41.8 7.4 %copy-start.2 = (s32[8]{0:T(128)S(1)}, s32[8]{0:T(128)}, u32[]{:S(2)}) copy-start(s32[8]{0:T(128)} %param.12) | copy-start | bytes 100
  43.7 52.3 %all-to-all-start.1 = ((bf16[16,2,2,128,128]{4,3,2,1,0:T(8,128)(2,1)}), bf16[16,2,2,128,128]{4,3,2,1,0:T(8,128)(2,1)S(1)}, u32[]{:S(2)}, u32[]{:S(2)}) async-start(bf16[16,2,2,128,128]{4,3,2,1,0:T(8,128)(2,1)} %bitcast.24), calls=%async_computation.1 | async-start | bytes 4194304 | tf_op jit(solution)/shard_map/all_to_all | solution.py:40
  173.7 8.9 %collective-permute-start = (f32[64,1024]{1,0:T(8,128)S(1)}, f32[64,1024]{1,0:T(8,128)S(1)}, u32[]{:S(2)}, u32[]{:S(2)}) collective-permute-start(f32[64,1024]{1,0:T(8,128)S(1)} %fusion.19), channel_id=1, source_target_pairs={{0,1},{1,0},{2,3},{3,2},{4,5},{5,4},{6,7},{7,6},{8,9},{9,8},{10,11... | collective-permute-start | bytes 786440 | tf_op jit(solution)/shard_map/ppermute | solution.py:88
  182.7 7.6 %collective-permute-start.1 = (f32[64,1024]{1,0:T(8,128)S(1)}, f32[64,1024]{1,0:T(8,128)S(1)}, u32[]{:S(2)}, u32[]{:S(2)}) collective-permute-start(f32[64,1024]{1,0:T(8,128)S(1)} %add.55), channel_id=1, source_target_pairs={{0,2},{1,3},{2,0},{3,1},{4,6},{5,7},{6,4},{7,5},{8,10},{9,11},{10,... | collective-permute-start | bytes 786440 | tf_op jit(solution)/shard_map/ppermute | solution.py:88
